TPU v7x, 32 devices: a whole 2x2x4 slice. The times are simulated.
32 devices in a mesh: sec: 4 (over y, x), gx: 4 (over z), gy: 2 (over core).
Axes of the slice: x: 2, y: 2, z: 4, core: 2. Of those that a mesh axis runs over, the one named last changes fastest.
Arguments:
- driving: float32 [3, 128, 256], P(None, 'gx', 'gy'), may hold values from -6 to 6
- rate_factor: float32 [3, 128, 256], P(None, 'gx', 'gy'), may hold values from 0.5 to 4
- friction_init: float32 [3, 128, 256], P(None, 'gx', 'gy'), may hold values from 0.2 to 2
- ice_mask: int32 [3, 128, 256], P(None, 'gx', 'gy'), may hold values 0 or 1
- grounded_mask: int32 [3, 128, 256], P(None, 'gx', 'gy'), may hold values 0 or 1
- melt: float32 [3, 128, 256], P(None, 'gx', 'gy'), may hold values from 0.1 to 1
- transmissivity: float32 [3, 128, 256], P(None, 'gx', 'gy'), may hold values from 0.5 to 5
- leakage: float32 [3, 128, 256], P(None, 'gx', 'gy'), may hold values from 0.05 to 0.5
- overburden: float32 [3, 128, 256], P(None, 'gx', 'gy'), may hold values from 0.5 to 2
- friction_scale: float32 [3, 128, 256], P(None, 'gx', 'gy'), may hold values from 0.5 to 4
Outputs:
- column_out: float32 [4, 3, 128, 256], P('sec', None, 'gx', 'gy')
All inputs are finite; a program needn't handle non-finite values. No bound on the sum of `ice_mask` or of `grounded_mask` on one device may be relied on, other than what follows from the above.
Results may differ from a plain program's by a relative error of at most 0.00002.
Values sent between devices are 32-bit elements; how exact they have to be, the bound alone decides.
A program may use at most 64 MiB of HBM per device.

v0:
```python
import functools

import jax
import jax.numpy as jnp
import numpy as np
from jax import lax
from jax.experimental import pallas as pl
from jax.experimental.pallas import tpu as pltpu
from jax.sharding import PartitionSpec as P

LAYERS = 40
SWEEPS = 4
VERT = 4.0
FLOOR = 0.25
HEATING = 0.5

RIM = 8
HALF = RIM // 2
RESCALE = 10
THIRD = -1.0 / (3.0 * float(np.log(2.0)))
DIRECTIONS = [(dx, dy) for dx in (-1, 0, 1) for dy in (-1, 0, 1) if (dx, dy) != (0, 0)]
MESH = pl.DeviceIdType.MESH


def basal_response():
    matrix = np.zeros((LAYERS, LAYERS))
    for k in range(LAYERS):
        matrix[k, k] = 4.0 + (VERT if k > 0 else 0.0) + (VERT if k < LAYERS - 1 else 0.0)
        if k > 0:
            matrix[k, k - 1] = matrix[k - 1, k] = -VERT
    unit = np.zeros(LAYERS)
    unit[0] = 1.0
    return np.linalg.solve(matrix, unit)


def turn(values, shift, axis):
    return pltpu.roll(values, shift % values.shape[axis], axis)


def neighbours(f):
    return turn(f, -1, 0), turn(f, 1, 0), turn(f, -1, 1), turn(f, 1, 1)


def water_solve(pressure, trans_eff, leakage, source, valid):
    faces = [0.5 * (trans_eff + t) for t in neighbours(trans_eff)]
    total = leakage + ((faces[0] + faces[1]) + (faces[2] + faces[3]))
    inverse = jnp.where(valid, 1.0 / total, 0.0)
    weights = [f * inverse for f in faces]
    base = source * inverse
    for _ in range(SWEEPS):
        parts = [w * p for w, p in zip(weights, neighbours(pressure))]
        pressure = base + ((parts[0] + parts[1]) + (parts[2] + parts[3]))
    return pressure


def kernel(sectors, nx, ny, *refs):
    ins = refs[:10]
    out = refs[10]
    floats, ints, pack_l, pack_r, rim_l, rim_r, q_ref, g_ref, r_ref, send_p = refs[11:21]
    in_sem, send_sem, recv_sem, last_send, last_recv = refs[21:]
    rows, lanes = ins[0].shape[1:]
    sec = lax.axis_index("sec")
    gx = lax.axis_index("gx")
    gy = lax.axis_index("gy")
    strip = lax.rem(sec, sectors)
    is_ice = sec < sectors
    sends_last = jnp.logical_and(sec > 0, is_ice)

    def exists(dx, dy):
        x, y = gx + dx, gy + dy
        return jnp.logical_and(
            jnp.logical_and(x >= 0, x < nx), jnp.logical_and(y >= 0, y < ny)
        )

    float_ids = (0, 1, 2, 5, 6, 7, 8, 9)
    int_ids = (3, 4)
    loads = []
    for slot, arg in enumerate(float_ids):
        loads.append(pltpu.make_async_copy(ins[arg].at[strip], floats.at[slot, pl.ds(RIM, rows)], in_sem.at[0]))
    for slot, arg in enumerate(int_ids):
        loads.append(pltpu.make_async_copy(ins[arg].at[strip], ints.at[slot, pl.ds(RIM, rows)], in_sem.at[1]))
    barrier = pltpu.get_barrier_semaphore()
    count = jnp.int32(0)
    for dx, dy in sorted(DIRECTIONS, key=lambda d: -abs(d[0])):
        here = exists(dx, dy)
        count = count + here.astype(jnp.int32)

        @pl.when(here)
        def _(dx=dx, dy=dy):
            pl.semaphore_signal(barrier, inc=1, device_id={"gx": gx + dx, "gy": gy + dy}, device_id_type=MESH)

    count = count + sends_last.astype(jnp.int32)
    count = count + jnp.where(is_ice, 0, sectors - 1)

    @pl.when(sends_last)
    def _():
        pl.semaphore_signal(barrier, inc=1, device_id={"sec": sectors}, device_id_type=MESH)

    for s in range(1, sectors):

        @pl.when(jnp.logical_not(is_ice))
        def _(s=s):
            pl.semaphore_signal(barrier, inc=1, device_id={"sec": s}, device_id_type=MESH)

    for load in loads:
        load.start()
    for slot, buffer in enumerate((floats, ints)):
        mine = buffer.at[:, pl.ds(RIM, rows)]
        pltpu.make_async_copy(mine, mine, in_sem.at[slot]).wait()

    lane = lax.broadcasted_iota(jnp.int32, (rows, lanes), 1)
    fields = [floats[i, RIM : RIM + rows] for i in range(8)]
    fields += [ints[i, RIM : RIM + rows].astype(jnp.float32) for i in range(2)]
    left = jnp.zeros((rows, lanes), jnp.float32)
    right = jnp.zeros((rows, lanes), jnp.float32)
    for i, f in enumerate(fields):
        moved = turn(f, RIM * i, 1)
        group = lane // RIM
        left = jnp.where(group == i, moved, left)
        right = jnp.where(group == (i - 1) % (lanes // RIM), moved, right)
    pack_l[...] = left
    pack_r[...] = right

    pl.semaphore_wait(barrier, count)

    def copies(dx, dy, n):
        target = {"gx": gx + dx, "gy": gy + dy}

        def remote(src, dst, m):
            return pltpu.make_async_remote_copy(
                src_ref=src, dst_ref=dst, send_sem=send_sem.at[m], recv_sem=recv_sem.at[m],
                device_id=target, device_id_type=MESH,
            )

        if dy == 0:
            first = rows if dx > 0 else RIM
            landing = 0 if dx > 0 else RIM + rows
            return [
                remote(floats.at[:, pl.ds(first, RIM)], floats.at[:, pl.ds(landing, RIM)], n),
                remote(ints.at[:, pl.ds(first, RIM)], ints.at[:, pl.ds(landing, RIM)], 8 + (dx > 0)),
            ]
        src, dst = (pack_r, rim_l) if dy > 0 else (pack_l, rim_r)
        if dx == 0:
            return [remote(src, dst.at[pl.ds(RIM, rows)], n)]
        first = rows - RIM if dx > 0 else 0
        landing = 0 if dx > 0 else RIM + rows
        return [remote(src.at[pl.ds(first, RIM)], dst.at[pl.ds(landing, RIM)], n)]

    order = sorted(range(8), key=lambda n: abs(DIRECTIONS[n][1]))
    for n in order:
        dx, dy = DIRECTIONS[n]

        @pl.when(exists(dx, dy))
        def _(dx=dx, dy=dy, n=n):
            for c in copies(dx, dy, n):
                c.start()

    def arrive(n):
        dx, dy = DIRECTIONS[n]

        @pl.when(exists(-dx, -dy))
        def _():
            for c in copies(dx, dy, n):
                c.wait_recv()

    w = basal_response()
    ext = rows + 2 * RIM
    tall = rows + RIM
    tiles = tall // 8
    wide = 2 * RIM
    slot = lax.broadcasted_iota(jnp.int32, (8, lanes), 1) // wide
    lane_low = jnp.where(gy < ny - 1, lanes + RIM, lanes)
    lane_high = jnp.where(gy > 0, 2 * lanes - RIM, 2 * lanes)

    def in_map_lanes(height):
        lane_i = lax.broadcasted_iota(jnp.int32, (height, 2 * lanes), 1)
        return jnp.logical_or(lane_i < lane_low, lane_i >= lane_high)

    def field_reader(top, height, valid):
        at = slice(top, top + height)
        packed_l, packed_r = rim_l[at], rim_r[at]
        group = lax.broadcasted_iota(jnp.int32, (height, lanes), 1) // RIM

        def field(i, fill):
            main = floats[i, at] if i < 8 else ints[i - 8, at].astype(jnp.float32)
            rim = turn(jnp.where(group == i, packed_r, packed_l), -RIM * i, 1)
            return jnp.where(valid, jnp.concatenate([main, rim], axis=1), fill)

        return field

    def first_velocity(driving, rate, friction, ice):
        viscous = rate * float(FLOOR ** (-1.0 / 3.0))
        speed = driving / (4.0 * viscous)
        drop = -speed * friction / (viscous + friction * float(w[0]))
        return speed * ice, drop * ice

    def squeeze(f, which):
        tile = jnp.zeros((8, lanes), jnp.float32)
        for n, t in enumerate(which):
            moved = turn(f[8 * t : 8 * t + 8, lanes:], wide * n + RIM, 1)
            tile = jnp.where(slot == n, moved, tile)
        return jnp.concatenate([f[8 * t : 8 * t + 8, :lanes] for t in which] + [tile], axis=0)

    def spread(f, count):
        last = f[8 * count :]
        return [
            jnp.concatenate([f[8 * n : 8 * n + 8], turn(last, -(wide * n + RIM), 1)], axis=1)
            for n in range(count)
        ]

    def eliminate(speed, drop, driving, rate, which, offset, lead):
        sxp, sxm, syp, sym = neighbours(speed)
        dxp, dxm, dyp, dym = neighbours(drop)
        sdx, sdy, ddx, ddy = sxp - sxm, syp - sym, dxp - dxm, dyp - dym
        flat = [
            0.03125 * (sdx * sdx + sdy * sdy) + 0.125 * FLOOR,
            0.0625 * (sdx * ddx + sdy * ddy),
            0.03125 * (ddx * ddx + ddy * ddy),
            0.125 * drop * drop,
            0.25 * ((sxp + sxm) + (syp + sym)),
            0.25 * ((dxp + dxm) + (dyp + dym)),
            driving * (0.5 / rate),
        ]
        flat = [squeeze(turn(f, lead, 0), which) for f in flat]
        for n in range(len(which) + 1):
            at = slice(offset + 8 * n, offset + 8 * n + 8)
            c0, c1, c2, c3, n0, n1, dr = [f[8 * n : 8 * n + 8] for f in flat]
            before = None
            for k in range(LAYERS):
                wk = float(w[k])
                strain = c0 + (c1 * wk + c2 * (wk * wk))
                if k < LAYERS - 1:
                    strain = strain + c3 * float((w[k + 1] - w[k]) ** 2)
                twice = jnp.exp2(jnp.log(strain) * THIRD)
                q_ref[k, at] = twice
                r_ref[k, at] = dr + twice * (n0 + n1 * wk)
                if k > 0:
                    g_ref[k - 1, at] = 0.5 * (before + twice)
                before = twice

        at = slice(offset, offset + 8 * (len(which) + 1))
        up_d, up_e, up_t = None, q_ref[0, at], r_ref[0, at]
        down_d, down_e, down_t = None, q_ref[LAYERS - 1, at], r_ref[LAYERS - 1, at]
        product = None

        def step(d, e, t, g, q, r):
            d = e + (g if d is None else g * d)
            return d, q * d + g * e, r * d + g * t

        for k in range(LAYERS - 1):
            j = LAYERS - 2 - k
            g = g_ref[k, at]
            product = g if product is None else product * g
            up_d, up_e, up_t = step(up_d, up_e, up_t, g, q_ref[k + 1, at], r_ref[k + 1, at])
            down_d, down_e, down_t = step(
                down_d, down_e, down_t, g_ref[j, at], q_ref[j, at], r_ref[j, at]
            )
            if k % RESCALE == RESCALE - 1 and k < LAYERS - 2:
                shrink = 1.0 / up_d
                up_d, up_e, up_t, product = None, up_e * shrink, up_t * shrink, product * shrink
                shrink = 1.0 / down_d
                down_d, down_e, down_t = None, down_e * shrink, down_t * shrink
        shrink = 1.0 / up_e
        return down_d, down_e, down_t, up_t * shrink, product * shrink

    def finish(parts, friction, rate, ice, which):
        down_d, down_e, down_t, top, reach = parts
        base = squeeze(turn(friction * (0.5 / rate), -HALF, 0), which)
        mask = squeeze(turn(ice, -HALF, 0), which)
        basal = down_t / (down_e + base * down_d)
        surface = top - base * basal * reach
        return [spread(f * mask, len(which)) for f in (basal, surface)]

    for n in order:
        if DIRECTIONS[n][0] == 0:
            arrive(n)
    early = list(range(1, tiles - 1))
    late = [0, tiles - 1]
    field = field_reader(RIM, rows, in_map_lanes(rows))
    driving, rate = field(0, 0.0), field(1, 1.0)
    speed, drop = first_velocity(driving, rate, field(2, 0.0) * field(9, 0.0), field(8, 0.0))
    early_parts = eliminate(speed, drop, driving, rate, early, 0, HALF)
    for n in order:
        if DIRECTIONS[n][0] != 0:
            arrive(n)

    row_i = lax.broadcasted_iota(jnp.int32, (ext, 2 * lanes), 0)
    row_low = jnp.where(gx > 0, 0, RIM)
    row_high = jnp.where(gx < nx - 1, ext, RIM + rows)
    valid = jnp.logical_and(
        jnp.logical_and(row_i >= row_low, row_i < row_high), in_map_lanes(ext)
    )
    field = field_reader(0, ext, valid)
    driving = field(0, 0.0)
    rate = field(1, 1.0)
    friction = field(2, 0.0)
    melt = field(3, 0.0)
    trans = field(4, 0.0)
    leakage = field(5, 1.0)
    pressure = field(6, 0.0)
    scale = field(7, 0.0)
    ice = field(8, 0.0)
    grounded = field(9, 0.0)
    friction = friction * grounded
    scale = scale * grounded

    speed, drop = first_velocity(driving, rate, friction, ice)
    sliding = speed + drop * float(w[0])
    squared = sliding * sliding
    trans_eff = trans * (1.0 + squared / (1.0 + squared))
    source = melt + HEATING * friction * squared
    pressure = water_solve(pressure, trans_eff, leakage, source, valid)
    friction = scale * pressure

    late_parts = eliminate(speed, drop, driving, rate, late, 8 * (len(early) + 1), -HALF)
    pieces = [None] * tiles
    for parts, which in ((early_parts, early), (late_parts, late)):
        for n, piece in enumerate(zip(*finish(parts, friction, rate, ice, which))):
            pieces[which[n]] = piece
    blank = jnp.zeros((RIM, 2 * lanes), jnp.float32)
    basal = turn(jnp.concatenate([p[0] for p in pieces] + [blank], axis=0), HALF, 0)
    surface = jnp.concatenate([p[1][:, :lanes] for p in pieces], axis=0)
    sliding = jnp.where(valid, basal, 0.0)
    squared = sliding * sliding
    trans_eff = trans * (1.0 + squared / (1.0 + squared))
    source = melt + HEATING * friction * squared
    pressure = water_solve(pressure, trans_eff, leakage, source, valid)
    block = pressure[RIM : RIM + rows, :lanes]
    send_p[...] = block

    def last():
        return pltpu.make_async_remote_copy(
            src_ref=send_p, dst_ref=out.at[0, strip], send_sem=last_send, recv_sem=last_recv.at[strip],
            device_id={"sec": sectors}, device_id_type=MESH,
        )

    @pl.when(sends_last)
    def _():
        last().start()

    @pl.when(is_ice)
    def _():
        out[0, 0] = turn(surface, -HALF, 0)[:rows]
        out[0, 1] = sliding[RIM : RIM + rows, :lanes]
        out[0, 2] = scale[RIM : RIM + rows, :lanes] * block

    @pl.when(jnp.logical_not(is_ice))
    def _():
        out[0, 0] = block

    for n in order:
        dx, dy = DIRECTIONS[n]

        @pl.when(exists(dx, dy))
        def _(dx=dx, dy=dy, n=n):
            for c in copies(dx, dy, n):
                c.wait_send()

    @pl.when(sends_last)
    def _():
        last().wait_send()

    for s in range(1, sectors):

        @pl.when(jnp.logical_not(is_ice))
        def _(s=s):
            pltpu.make_async_remote_copy(
                src_ref=send_p, dst_ref=out.at[0, s], send_sem=last_send, recv_sem=last_recv.at[s],
                device_id={"sec": 0}, device_id_type=MESH,
            ).wait_recv()


def on_device(nx, ny, *args):
    sectors, rows, lanes = args[0].shape
    ext = rows + 2 * RIM
    f32 = jnp.float32
    vmem = pltpu.VMEM
    dma = pltpu.SemaphoreType.DMA
    return pl.pallas_call(
        functools.partial(kernel, sectors, nx, ny),
        out_shape=pltpu.VMEM((1, sectors, rows, lanes), f32),
        in_specs=[pl.BlockSpec(memory_space=pltpu.HBM)] * len(args),
        out_specs=pl.BlockSpec(memory_space=pltpu.VMEM),
        scratch_shapes=[
            vmem((8, ext, lanes), f32),
            vmem((2, ext, lanes), jnp.int32),
            vmem((rows, lanes), f32),
            vmem((rows, lanes), f32),
            vmem((ext, lanes), f32),
            vmem((ext, lanes), f32),
            vmem((LAYERS, ext + RIM, lanes), f32),
            vmem((LAYERS, ext + RIM, lanes), f32),
            vmem((LAYERS, ext + RIM, lanes), f32),
            vmem((rows, lanes), f32),
            dma((2,)),
            dma((10,)),
            dma((10,)),
            dma,
            dma((sectors,)),
        ],
        compiler_params=pltpu.CompilerParams(collective_id=0, has_side_effects=True),
    )(*args)


def solution(mesh):
    spec = P(None, "gx", "gy")
    return jax.shard_map(
        functools.partial(on_device, mesh.shape["gx"], mesh.shape["gy"]),
        mesh=mesh,
        in_specs=(spec,) * 10,
        out_specs=P("sec", None, "gx", "gy"),
        check_vma=False,
    )
```

profile of v0, /device:TPU:14, one launch (start us, length us, event | category | flops | bytes accessed | tf_op | source)
XLA Modules:
  0.0 9.6 jit_solution(5890244333465779979)
XLA Ops:
  0.0 9.0 %shard_map.100 = f32[1,3,32,128]{3,2,1,0:T(8,128)S(1)} custom-call(f32[3,32,128]{2,1,0:T(8,128)} %refs_0_.1, f32[3,32,128]{2,1,0:T(8,128)} %refs_1_.1, f32[3,32,128]{2,1,0:T(8,128)} %refs_2_.1, s32[3,32,128]{2,1,0:T(8,128)} %refs_3_.1, s32[3,32,128]{2,1,0:T(8,128)} %refs_4_.1, f32[3,32,128]{2,1,0:T(8,128)} %refs_5_.1, f32[3,32,128]{2,1,0:T(8,128)} %refs_6_.1, ...), custom_call_target="tpu_custom_call" | custom-call | tf_op jit(solution)/shard_map/pallas_call | solution.py:379
  9.0 0.6 %copy.12 = f32[1,3,32,128]{3,2,1,0:T(8,128)} copy(f32[1,3,32,128]{3,2,1,0:T(8,128)S(1)} %shard_map.100) | data formatting | bytes 98304
where the time goes:
time: 9.81 us; the launch traced here: 9.64 us
  Pallas kernels  9.01 us (92%)
  local copies, waits for them, and re-layouts  0.62 us (6%)
    pallas_call x1, Pallas kernels, on_device(): pl.pallas_call(functools.partial(kernel, sectors, nx, ny), out_shape=pltp...  9.01 us
    unnamed x1, local copies, waits for them, and re-layouts  0.62 us

commit v1 on v0

--- a/solution.py
+++ b/solution.py
@@ -18,7 +18,6 @@
 HALF = RIM // 2
 RESCALE = 10
 THIRD = -1.0 / (3.0 * float(np.log(2.0)))
-DIRECTIONS = [(dx, dy) for dx in (-1, 0, 1) for dy in (-1, 0, 1) if (dx, dy) != (0, 0)]
 MESH = pl.DeviceIdType.MESH
 
 
@@ -56,121 +55,169 @@
 def kernel(sectors, nx, ny, *refs):
     ins = refs[:10]
     out = refs[10]
-    floats, ints, pack_l, pack_r, rim_l, rim_r, q_ref, g_ref, r_ref, send_p = refs[11:21]
-    in_sem, send_sem, recv_sem, last_send, last_recv = refs[21:]
+    own_f, own_i, floats, ints, near, far, pack_near, pack_far, q_ref, g_ref, r_ref, send_p, results = refs[11:24]
+    in_sem, send_sem, recv_sem, credit, out_send, out_recv = refs[24:]
     rows, lanes = ins[0].shape[1:]
+    ext = rows + 2 * RIM
+    wide_map = ny > 2
     sec = lax.axis_index("sec")
     gx = lax.axis_index("gx")
     gy = lax.axis_index("gy")
+    odd = lax.rem(gy, 2)
+    even = 1 - odd
+    is_odd = odd == 1
+    is_even = odd == 0
+    partner = gy + even - odd
+    far_to = gy + 2 * odd - 2 * even
+    far_from = gy + 2 * even - 2 * odd
     strip = lax.rem(sec, sectors)
     is_ice = sec < sectors
+    is_water = jnp.logical_not(is_ice)
     sends_last = jnp.logical_and(sec > 0, is_ice)
-
-    def exists(dx, dy):
-        x, y = gx + dx, gy + dy
-        return jnp.logical_and(
-            jnp.logical_and(x >= 0, x < nx), jnp.logical_and(y >= 0, y < ny)
-        )
+    below, above = gx > 0, gx < nx - 1
+
+    def in_map(y):
+        return jnp.logical_and(y >= 0, y < ny)
+
+    def both(*conditions):
+        return functools.reduce(jnp.logical_and, conditions)
+
+    def number(condition):
+        return condition.astype(jnp.int32)
 
     float_ids = (0, 1, 2, 5, 6, 7, 8, 9)
     int_ids = (3, 4)
-    loads = []
     for slot, arg in enumerate(float_ids):
-        loads.append(pltpu.make_async_copy(ins[arg].at[strip], floats.at[slot, pl.ds(RIM, rows)], in_sem.at[0]))
+        pltpu.make_async_copy(ins[arg].at[strip], own_f.at[slot], in_sem.at[0]).start()
     for slot, arg in enumerate(int_ids):
-        loads.append(pltpu.make_async_copy(ins[arg].at[strip], ints.at[slot, pl.ds(RIM, rows)], in_sem.at[1]))
+        pltpu.make_async_copy(ins[arg].at[strip], own_i.at[slot], in_sem.at[1]).start()
+
     barrier = pltpu.get_barrier_semaphore()
-    count = jnp.int32(0)
-    for dx, dy in sorted(DIRECTIONS, key=lambda d: -abs(d[0])):
-        here = exists(dx, dy)
-        count = count + here.astype(jnp.int32)
-
-        @pl.when(here)
-        def _(dx=dx, dy=dy):
-            pl.semaphore_signal(barrier, inc=1, device_id={"gx": gx + dx, "gy": gy + dy}, device_id_type=MESH)
-
-    count = count + sends_last.astype(jnp.int32)
-    count = count + jnp.where(is_ice, 0, sectors - 1)
-
-    @pl.when(sends_last)
+
+    def signal(condition, sem, target):
+        @pl.when(condition)
+        def _():
+            pl.semaphore_signal(sem, inc=1, device_id=target, device_id_type=MESH)
+
+    signal(above, barrier, {"gx": gx + 1, "gy": partner})
+    signal(above, barrier, {"gx": gx + 1})
+    signal(is_odd, barrier, {"gy": partner})
+    signal(sends_last, barrier, {"sec": sectors, "gy": partner})
+    count = number(is_even) + 2 * number(below) + jnp.where(is_ice, 0, sectors - 1)
+    if wide_map:
+        for y in (gy - 2, gy + 2):
+            signal(both(above, in_map(y)), barrier, {"gx": gx + 1, "gy": y})
+            count = count + number(both(below, in_map(y)))
+        signal(in_map(gy + 2), barrier, {"gy": gy + 2})
+        count = count + number(in_map(gy - 2))
+
+    @pl.when(count > 0)
     def _():
-        pl.semaphore_signal(barrier, inc=1, device_id={"sec": sectors}, device_id_type=MESH)
-
+        pl.semaphore_wait(barrier, count)
+
+    signal(below, credit.at[0], {"gx": gx - 1, "gy": partner})
+    signal(below, credit.at[0], {"gx": gx - 1})
+    signal(is_even, credit.at[1], {"gy": partner})
     for s in range(1, sectors):
-
-        @pl.when(jnp.logical_not(is_ice))
-        def _(s=s):
-            pl.semaphore_signal(barrier, inc=1, device_id={"sec": s}, device_id_type=MESH)
-
-    for load in loads:
-        load.start()
-    for slot, buffer in enumerate((floats, ints)):
-        mine = buffer.at[:, pl.ds(RIM, rows)]
-        pltpu.make_async_copy(mine, mine, in_sem.at[slot]).wait()
-
-    lane = lax.broadcasted_iota(jnp.int32, (rows, lanes), 1)
-    fields = [floats[i, RIM : RIM + rows] for i in range(8)]
-    fields += [ints[i, RIM : RIM + rows].astype(jnp.float32) for i in range(2)]
-    left = jnp.zeros((rows, lanes), jnp.float32)
-    right = jnp.zeros((rows, lanes), jnp.float32)
-    for i, f in enumerate(fields):
-        moved = turn(f, RIM * i, 1)
-        group = lane // RIM
-        left = jnp.where(group == i, moved, left)
-        right = jnp.where(group == (i - 1) % (lanes // RIM), moved, right)
-    pack_l[...] = left
-    pack_r[...] = right
-
-    pl.semaphore_wait(barrier, count)
-
-    def copies(dx, dy, n):
-        target = {"gx": gx + dx, "gy": gy + dy}
-
-        def remote(src, dst, m):
-            return pltpu.make_async_remote_copy(
-                src_ref=src, dst_ref=dst, send_sem=send_sem.at[m], recv_sem=recv_sem.at[m],
-                device_id=target, device_id_type=MESH,
-            )
-
-        if dy == 0:
-            first = rows if dx > 0 else RIM
-            landing = 0 if dx > 0 else RIM + rows
-            return [
-                remote(floats.at[:, pl.ds(first, RIM)], floats.at[:, pl.ds(landing, RIM)], n),
-                remote(ints.at[:, pl.ds(first, RIM)], ints.at[:, pl.ds(landing, RIM)], 8 + (dx > 0)),
-            ]
-        src, dst = (pack_r, rim_l) if dy > 0 else (pack_l, rim_r)
-        if dx == 0:
-            return [remote(src, dst.at[pl.ds(RIM, rows)], n)]
-        first = rows - RIM if dx > 0 else 0
-        landing = 0 if dx > 0 else RIM + rows
-        return [remote(src.at[pl.ds(first, RIM)], dst.at[pl.ds(landing, RIM)], n)]
-
-    order = sorted(range(8), key=lambda n: abs(DIRECTIONS[n][1]))
-    for n in order:
-        dx, dy = DIRECTIONS[n]
-
-        @pl.when(exists(dx, dy))
-        def _(dx=dx, dy=dy, n=n):
-            for c in copies(dx, dy, n):
+        signal(is_water, credit.at[3], {"sec": s, "gy": partner})
+    if wide_map:
+        signal(both(below, in_map(far_from)), credit.at[0], {"gx": gx - 1, "gy": far_from})
+        signal(both(is_odd, in_map(gy - 2)), credit.at[2], {"gy": gy - 2})
+
+    for sem, buffer in enumerate((own_f, own_i)):
+        pltpu.make_async_copy(buffer, buffer, in_sem.at[sem]).wait()
+
+    def remote(src, dst, m, target):
+        return pltpu.make_async_remote_copy(
+            src_ref=src, dst_ref=dst, send_sem=send_sem.at[m], recv_sem=recv_sem.at[m],
+            device_id=target, device_id_type=MESH,
+        )
+
+    def main_copies():
+        target = {"gy": partner}
+        at = pl.ds(RIM, rows)
+        return [remote(own_f, floats.at[:, at], 0, target), remote(own_i, ints.at[:, at], 1, target)]
+
+    def edge_copies(dx):
+        target = {"gx": gx + dx, "gy": partner}
+        src = pl.ds(rows - RIM if dx > 0 else 0, RIM)
+        dst = pl.ds(0 if dx > 0 else RIM + rows, RIM)
+        m = 2 + 2 * (dx > 0)
+        return [
+            remote(own_f.at[:, src], floats.at[:, dst], m, target),
+            remote(own_i.at[:, src], ints.at[:, dst], m + 1, target),
+        ]
+
+    def corner_copy(dx):
+        return remote(
+            pack_near.at[int(dx > 0)], near.at[int(dx < 0)], 6 + (dx > 0), {"gx": gx + dx}
+        )
+
+    def far_copy(dx):
+        src = pl.ds({-1: 0, 0: 0, 1: rows - RIM}[dx], rows if dx == 0 else RIM)
+        dst = pl.ds({-1: RIM + rows, 0: RIM, 1: 0}[dx], rows if dx == 0 else RIM)
+        return remote(pack_far.at[src], far.at[dst], 9 + dx, {"gx": gx + dx, "gy": far_to})
+
+    def x_copies(dx):
+        return [*edge_copies(dx), corner_copy(dx)]
+
+    def pack(top, height, parity):
+        group = (lax.broadcasted_iota(jnp.int32, (height, lanes), 1) // RIM + parity) % (lanes // RIM)
+        packed = jnp.zeros((height, lanes), jnp.float32)
+        for i in range(10):
+            f = own_f[i, top : top + height] if i < 8 else own_i[i - 8, top : top + height].astype(jnp.float32)
+            packed = jnp.where(group == i, turn(f, RIM * i, 1), packed)
+        return packed
+
+    pack_near[0] = pack(0, RIM, even)
+    pack_near[1] = pack(rows - RIM, RIM, even)
+    if wide_map:
+        pack_far[...] = pack(0, rows, odd)
+
+    def start(condition, copies):
+        @pl.when(condition)
+        def _():
+            for c in copies:
                 c.start()
 
-    def arrive(n):
-        dx, dy = DIRECTIONS[n]
-
-        @pl.when(exists(-dx, -dy))
+    def wait_send(condition, copies):
+        @pl.when(condition)
         def _():
-            for c in copies(dx, dy, n):
+            for c in copies:
+                c.wait_send()
+
+    def arrive(condition, copies):
+        @pl.when(condition)
+        def _():
+            for c in copies:
                 c.wait_recv()
 
+    def await_credit(condition, which, amount):
+        @pl.when(condition)
+        def _():
+            pl.semaphore_wait(credit.at[which], amount)
+
+    start(below, x_copies(-1))
+    if wide_map:
+        start(both(below, in_map(far_to)), [far_copy(-1)])
+    await_credit(is_odd, 1, 1)
+    for c in main_copies():
+        c.start()
+    if wide_map:
+        await_credit(both(is_odd, in_map(far_to)), 2, 1)
+        start(in_map(far_to), [far_copy(0)])
+    await_credit(above, 0, 2 + number(in_map(far_to)) if wide_map else 2)
+    start(above, x_copies(1))
+    if wide_map:
+        start(both(above, in_map(far_to)), [far_copy(1)])
+
     w = basal_response()
-    ext = rows + 2 * RIM
     tall = rows + RIM
     tiles = tall // 8
     wide = 2 * RIM
     slot = lax.broadcasted_iota(jnp.int32, (8, lanes), 1) // wide
-    lane_low = jnp.where(gy < ny - 1, lanes + RIM, lanes)
-    lane_high = jnp.where(gy > 0, 2 * lanes - RIM, 2 * lanes)
+    lane_low = jnp.where(partner < ny - 1, lanes + RIM, lanes)
+    lane_high = jnp.where(partner > 0, 2 * lanes - RIM, 2 * lanes)
 
     def in_map_lanes(height):
         lane_i = lax.broadcasted_iota(jnp.int32, (height, 2 * lanes), 1)
@@ -178,12 +225,16 @@
 
     def field_reader(top, height, valid):
         at = slice(top, top + height)
-        packed_l, packed_r = rim_l[at], rim_r[at]
-        group = lax.broadcasted_iota(jnp.int32, (height, lanes), 1) // RIM
+        lane = lax.broadcasted_iota(jnp.int32, (height, lanes), 1)
+        is_near = (lane >= lanes // 2) == is_even
 
         def field(i, fill):
             main = floats[i, at] if i < 8 else ints[i - 8, at].astype(jnp.float32)
-            rim = turn(jnp.where(group == i, packed_r, packed_l), -RIM * i, 1)
+            rim = own_f[i] if i < 8 else own_i[i - 8].astype(jnp.float32)
+            if height > rows:
+                rim = jnp.concatenate([turn(near[0], -RIM * i, 1), rim, turn(near[1], -RIM * i, 1)], axis=0)
+            if wide_map:
+                rim = jnp.where(is_near, rim, turn(far[at], -RIM * i, 1))
             return jnp.where(valid, jnp.concatenate([main, rim], axis=1), fill)
 
         return field
@@ -271,18 +322,19 @@
         surface = top - base * basal * reach
         return [spread(f * mask, len(which)) for f in (basal, surface)]
 
-    for n in order:
-        if DIRECTIONS[n][0] == 0:
-            arrive(n)
+    arrive(gx >= 0, main_copies())
+    if wide_map:
+        arrive(in_map(far_from), [far_copy(0)])
     early = list(range(1, tiles - 1))
     late = [0, tiles - 1]
     field = field_reader(RIM, rows, in_map_lanes(rows))
     driving, rate = field(0, 0.0), field(1, 1.0)
     speed, drop = first_velocity(driving, rate, field(2, 0.0) * field(9, 0.0), field(8, 0.0))
     early_parts = eliminate(speed, drop, driving, rate, early, 0, HALF)
-    for n in order:
-        if DIRECTIONS[n][0] != 0:
-            arrive(n)
+    for dx, condition in ((-1, above), (1, below)):
+        arrive(condition, x_copies(dx))
+        if wide_map:
+            arrive(both(condition, in_map(far_from)), [far_copy(dx)])
 
     row_i = lax.broadcasted_iota(jnp.int32, (ext, 2 * lanes), 0)
     row_low = jnp.where(gx > 0, 0, RIM)
@@ -328,46 +380,46 @@
     block = pressure[RIM : RIM + rows, :lanes]
     send_p[...] = block
 
-    def last():
+    def result_copy(src, plane, m, target):
         return pltpu.make_async_remote_copy(
-            src_ref=send_p, dst_ref=out.at[0, strip], send_sem=last_send, recv_sem=last_recv.at[strip],
-            device_id={"sec": sectors}, device_id_type=MESH,
+            src_ref=src, dst_ref=out.at[0, plane], send_sem=out_send.at[m], recv_sem=out_recv.at[plane],
+            device_id=target, device_id_type=MESH,
         )
 
-    @pl.when(sends_last)
-    def _():
-        last().start()
+    def water_copy():
+        return result_copy(send_p, strip, sectors, {"sec": sectors, "gy": partner})
+
+    def own_copy():
+        return result_copy(send_p, 0, 0, {"gy": partner})
+
+    def ice_copies():
+        return [result_copy(results.at[n], n, n, {"gy": partner}) for n in range(3)]
+
+    await_credit(sends_last, 3, 1)
+    start(sends_last, [water_copy()])
+    start(is_water, [own_copy()])
 
     @pl.when(is_ice)
     def _():
-        out[0, 0] = turn(surface, -HALF, 0)[:rows]
-        out[0, 1] = sliding[RIM : RIM + rows, :lanes]
-        out[0, 2] = scale[RIM : RIM + rows, :lanes] * block
-
-    @pl.when(jnp.logical_not(is_ice))
-    def _():
-        out[0, 0] = block
-
-    for n in order:
-        dx, dy = DIRECTIONS[n]
-
-        @pl.when(exists(dx, dy))
-        def _(dx=dx, dy=dy, n=n):
-            for c in copies(dx, dy, n):
-                c.wait_send()
-
-    @pl.when(sends_last)
-    def _():
-        last().wait_send()
-
-    for s in range(1, sectors):
-
-        @pl.when(jnp.logical_not(is_ice))
-        def _(s=s):
-            pltpu.make_async_remote_copy(
-                src_ref=send_p, dst_ref=out.at[0, s], send_sem=last_send, recv_sem=last_recv.at[s],
-                device_id={"sec": 0}, device_id_type=MESH,
-            ).wait_recv()
+        results[0] = turn(surface, -HALF, 0)[:rows]
+        results[1] = sliding[RIM : RIM + rows, :lanes]
+        results[2] = scale[RIM : RIM + rows, :lanes] * block
+        for c in ice_copies():
+            c.start()
+
+    for c in main_copies():
+        c.wait_send()
+    if wide_map:
+        wait_send(in_map(far_to), [far_copy(0)])
+    for dx, condition in ((-1, below), (1, above)):
+        wait_send(condition, x_copies(dx))
+        if wide_map:
+            wait_send(both(condition, in_map(far_to)), [far_copy(dx)])
+    wait_send(sends_last, [water_copy()])
+    wait_send(is_water, [own_copy()])
+    wait_send(is_ice, ice_copies())
+    for plane in range(3):
+        result_copy(send_p, plane, 0, {"gy": partner}).wait_recv()
 
 
 def on_device(nx, ny, *args):
@@ -382,21 +434,25 @@
         in_specs=[pl.BlockSpec(memory_space=pltpu.HBM)] * len(args),
         out_specs=pl.BlockSpec(memory_space=pltpu.VMEM),
         scratch_shapes=[
+            vmem((8, rows, lanes), f32),
+            vmem((2, rows, lanes), jnp.int32),
             vmem((8, ext, lanes), f32),
             vmem((2, ext, lanes), jnp.int32),
+            vmem((2, RIM, lanes), f32),
+            vmem((ext, lanes), f32),
+            vmem((2, RIM, lanes), f32),
             vmem((rows, lanes), f32),
-            vmem((rows, lanes), f32),
-            vmem((ext, lanes), f32),
-            vmem((ext, lanes), f32),
             vmem((LAYERS, ext + RIM, lanes), f32),
             vmem((LAYERS, ext + RIM, lanes), f32),
             vmem((LAYERS, ext + RIM, lanes), f32),
             vmem((rows, lanes), f32),
+            vmem((3, rows, lanes), f32),
             dma((2,)),
-            dma((10,)),
-            dma((10,)),
-            dma,
-            dma((sectors,)),
+            dma((11,)),
+            dma((11,)),
+            pltpu.SemaphoreType.REGULAR((4,)),
+            dma((4,)),
+            dma((3,)),
         ],
         compiler_params=pltpu.CompilerParams(collective_id=0, has_side_effects=True),
     )(*args)

time: 9.81 us -> 9.37 us (0.955)
  the two profiles are of different devices: /device:TPU:14 before, /device:TPU:0 now
where the time goes in v1:
time: 9.37 us; the launch traced here: 9.2 us
  Pallas kernels  8.57 us (91%)
  local copies, waits for them, and re-layouts  0.62 us (7%)
    pallas_call x1, Pallas kernels, on_device(): pl.pallas_call(functools.partial(kernel, sectors, nx, ny), out_shape=pltp...  8.57 us
    unnamed x1, local copies, waits for them, and re-layouts  0.62 us

profile of v1, /device:TPU:0, one launch (start us, length us, event | category | flops | bytes accessed | tf_op | source)
XLA Modules:
  0.0 9.2 jit_solution(3691548866776952564)
XLA Ops:
  0.0 8.6 %shard_map.100 = f32[1,3,32,128]{3,2,1,0:T(8,128)S(1)} custom-call(f32[3,32,128]{2,1,0:T(8,128)} %refs_0_.1, f32[3,32,128]{2,1,0:T(8,128)} %refs_1_.1, f32[3,32,128]{2,1,0:T(8,128)} %refs_2_.1, s32[3,32,128]{2,1,0:T(8,128)} %refs_3_.1, s32[3,32,128]{2,1,0:T(8,128)} %refs_4_.1, f32[3,32,128]{2,1,0:T(8,128)} %refs_5_.1, f32[3,32,128]{2,1,0:T(8,128)} %refs_6_.1, ...), custom_call_target="tpu_custom_call" | custom-call | tf_op jit(solution)/shard_map/pallas_call | solution.py:431
  8.6 0.6 %copy.12 = f32[1,3,32,128]{3,2,1,0:T(8,128)} copy(f32[1,3,32,128]{3,2,1,0:T(8,128)S(1)} %shard_map.100) | data formatting | bytes 98304

commit v2 on v0

--- a/solution.py
+++ b/solution.py
@@ -53,7 +53,7 @@
     return pressure
 
 
-def kernel(sectors, nx, ny, *refs):
+def wide_kernel(sectors, nx, ny, *refs):
     ins = refs[:10]
     out = refs[10]
     floats, ints, pack_l, pack_r, rim_l, rim_r, q_ref, g_ref, r_ref, send_p = refs[11:21]
@@ -370,14 +370,14 @@
             ).wait_recv()
 
 
-def on_device(nx, ny, *args):
+def wide_map(nx, ny, *args):
     sectors, rows, lanes = args[0].shape
     ext = rows + 2 * RIM
     f32 = jnp.float32
     vmem = pltpu.VMEM
     dma = pltpu.SemaphoreType.DMA
     return pl.pallas_call(
-        functools.partial(kernel, sectors, nx, ny),
+        functools.partial(wide_kernel, sectors, nx, ny),
         out_shape=pltpu.VMEM((1, sectors, rows, lanes), f32),
         in_specs=[pl.BlockSpec(memory_space=pltpu.HBM)] * len(args),
         out_specs=pl.BlockSpec(memory_space=pltpu.VMEM),
@@ -402,10 +402,422 @@
     )(*args)
 
 
+def narrow_kernel(sectors, nx, *refs):
+    ins = refs[:10]
+    out = refs[10]
+    own_f, own_i, part_f, part_i, halo_f, halo_i, q_ref, g_ref, r_ref, send_p, results = refs[11:22]
+    in_sem, send_sem, recv_sem, credit, out_send, out_recv = refs[22:]
+    rows, lanes = ins[0].shape[1:]
+    half = rows // 2
+    local = half + RIM
+    tiles = local // RIM
+    sec = lax.axis_index("sec")
+    gx = lax.axis_index("gx")
+    gy = lax.axis_index("gy")
+    partner = 1 - gy
+    is_odd = gy == 1
+    is_even = gy == 0
+    strip = lax.rem(sec, sectors)
+    is_ice = sec < sectors
+    is_water = jnp.logical_not(is_ice)
+    sends_last = jnp.logical_and(sec > 0, is_ice)
+    below, above = gx > 0, gx < nx - 1
+    low = jnp.where(sec == 0, 0, 1)
+    high = 1 - low
+    is_low = gy == low
+    is_high = gy == high
+    part_low = jnp.where(is_low, 0, rows - local)
+    has_halo = jnp.logical_or(jnp.logical_and(is_low, below), jnp.logical_and(is_high, above))
+
+    def both(p, q):
+        return jnp.logical_and(p, q)
+
+    def number(condition):
+        return condition.astype(jnp.int32)
+
+    def copy_in(n):
+        arg = (0, 1, 2, 5, 6, 7, 8, 9, 3, 4)[n]
+        dst = own_f.at[n] if n < 8 else own_i.at[n - 8]
+        return pltpu.make_async_copy(ins[arg].at[strip], dst, in_sem.at[int(n >= 8)])
+
+    for n in range(10):
+        copy_in(n).start()
+
+    barrier = pltpu.get_barrier_semaphore()
+
+    def signal(condition, sem, target):
+        @pl.when(condition)
+        def _():
+            pl.semaphore_signal(sem, inc=1, device_id=target, device_id_type=MESH)
+
+    signal(above, barrier, {"gx": gx + 1, "gy": low})
+    signal(both(above, is_high), barrier, {"gx": gx + 1, "gy": high})
+    signal(is_odd, barrier, {"gy": partner})
+    signal(sends_last, barrier, {"sec": sectors, "gy": partner})
+    signal(sends_last, barrier, {"sec": sectors})
+    count = number(is_even) + number(below) + number(both(below, is_low)) + jnp.where(is_ice, 0, 2 * (sectors - 1))
+
+    @pl.when(count > 0)
+    def _():
+        pl.semaphore_wait(barrier, count)
+
+    signal(both(below, is_low), credit.at[0], {"gx": gx - 1, "gy": partner})
+    signal(both(below, is_low), credit.at[0], {"gx": gx - 1})
+    signal(is_even, credit.at[1], {"gy": partner})
+    for s in range(1, sectors):
+        signal(is_water, credit.at[2], {"sec": s, "gy": partner})
+        signal(is_water, credit.at[2], {"sec": s})
+
+    for sem, buffer in enumerate((own_f, own_i)):
+        pltpu.make_async_copy(buffer, buffer, in_sem.at[sem]).wait()
+
+    def remote(src, dst, m, k, target):
+        return pltpu.make_async_remote_copy(
+            src_ref=src, dst_ref=dst, send_sem=send_sem.at[m], recv_sem=recv_sem.at[k],
+            device_id=target, device_id_type=MESH,
+        )
+
+    def main_copies():
+        at = pl.ds(pl.multiple_of(rows - local - part_low, RIM), local)
+        return [
+            remote(own_f.at[:, at], part_f, 0, 0, {"gy": partner}),
+            remote(own_i.at[:, at], part_i, 1, 1, {"gy": partner}),
+        ]
+
+    def edge_copies(dx, region):
+        src = pl.ds(half * (dx + 1) - RIM * (dx > 0), RIM)
+        target = {"gx": gx + dx, "gy": low if dx > 0 else high}
+        return [
+            remote(own_f.at[:, src], halo_f.at[region], 3 + dx, 2 + region, target),
+            remote(own_i.at[:, src], halo_i.at[region], 4 + dx, 4 + region, target),
+        ]
+
+    def start(condition, copies):
+        @pl.when(condition)
+        def _():
+            for c in copies:
+                c.start()
+
+    def wait_send(condition, copies):
+        @pl.when(condition)
+        def _():
+            for c in copies:
+                c.wait_send()
+
+    def await_credit(condition, which, amount):
+        @pl.when(condition)
+        def _():
+            pl.semaphore_wait(credit.at[which], amount)
+
+    start(below, edge_copies(-1, gy))
+    await_credit(is_odd, 1, 1)
+    for c in main_copies():
+        c.start()
+    await_credit(above, 0, 1)
+    start(above, edge_copies(1, gy))
+
+    w = basal_response()
+    wide = 2 * lanes
+    lane = lax.broadcasted_iota(jnp.int32, (RIM, wide), 1)
+    upper_sub = lax.broadcasted_iota(jnp.int32, (RIM, wide), 0) >= HALF
+    halo_in_late = upper_sub == is_low
+    edge = jnp.where(is_even, wide, lanes)
+    last_lane = lane == edge - 1
+    first_lane = lane == lax.rem(edge, wide)
+
+    def join(parts):
+        return jnp.concatenate(parts, axis=0)
+
+    def tall_mask(mask, count):
+        return join([mask] * count)
+
+    def field_local(i):
+        at = pl.ds(pl.multiple_of(part_low, RIM), local)
+        a = own_f[i, at] if i < 8 else own_i[i - 8, at].astype(jnp.float32)
+        b = part_f[i] if i < 8 else part_i[i - 8].astype(jnp.float32)
+        return jnp.concatenate([a, b], axis=1)
+
+    def field_halo(i, fill):
+        a, b = [halo_f[r, i] if i < 8 else halo_i[r, i - 8].astype(jnp.float32) for r in (gy, partner)]
+        return jnp.where(has_halo, jnp.concatenate([a, b], axis=1), fill)
+
+    def first_velocity(driving, rate, friction, ice):
+        viscous = rate * float(FLOOR ** (-1.0 / 3.0))
+        speed = driving / (4.0 * viscous)
+        drop = -speed * friction / (viscous + friction * float(w[0]))
+        return speed * ice, drop * ice
+
+    def shifts(f):
+        count = f.shape[0] // RIM
+        yp = jnp.where(tall_mask(last_lane, count), 0.0, turn(f, -1, 1))
+        ym = jnp.where(tall_mask(first_lane, count), 0.0, turn(f, 1, 1))
+        return turn(f, -1, 0), turn(f, 1, 0), yp, ym
+
+    def sheet(sliding, trans, melt, friction):
+        squared = sliding * sliding
+        return trans * (1.0 + squared / (1.0 + squared)), melt + HEATING * friction * squared
+
+    def water_solve(pressure, trans_eff, leakage, source, valid):
+        faces = [0.5 * (trans_eff + t) for t in shifts(trans_eff)]
+        total = leakage + ((faces[0] + faces[1]) + (faces[2] + faces[3]))
+        inverse = jnp.where(valid, 1.0 / total, 0.0)
+        weights = [f * inverse for f in faces]
+        count = pressure.shape[0] // RIM
+        weights[2] = jnp.where(tall_mask(last_lane, count), 0.0, weights[2])
+        weights[3] = jnp.where(tall_mask(first_lane, count), 0.0, weights[3])
+        base = source * inverse
+        for _ in range(SWEEPS):
+            parts = [w * p for w, p in zip(weights, neighbours(pressure))]
+            pressure = base + ((parts[0] + parts[1]) + (parts[2] + parts[3]))
+        return pressure
+
+    def between(f):
+        pieces = [f[RIM * k : RIM * k + RIM] for k in range(f.shape[0] // RIM)]
+        return join([jnp.where(upper_sub, p, q) for p, q in zip(pieces[:-1], pieces[1:])])
+
+    def late_tile(halo, first, last):
+        return jnp.where(halo_in_late, halo, jnp.where(is_low, first, last))
+
+    def coefficients(s_shift, d_shift, drop, driving, rate):
+        sdx, sdy = s_shift[0] - s_shift[1], s_shift[2] - s_shift[3]
+        ddx, ddy = d_shift[0] - d_shift[1], d_shift[2] - d_shift[3]
+        return [
+            0.03125 * (sdx * sdx + sdy * sdy) + 0.125 * FLOOR,
+            0.0625 * (sdx * ddx + sdy * ddy),
+            0.03125 * (ddx * ddx + ddy * ddy),
+            0.125 * drop * drop,
+            0.25 * ((s_shift[0] + s_shift[1]) + (s_shift[2] + s_shift[3])),
+            0.25 * ((d_shift[0] + d_shift[1]) + (d_shift[2] + d_shift[3])),
+            driving * (0.5 / rate),
+        ]
+
+    def viscosity(flat, offset):
+        for n in range(flat[0].shape[0] // RIM):
+            at = slice(offset + RIM * n, offset + RIM * n + RIM)
+            c0, c1, c2, c3, n0, n1, dr = [f[RIM * n : RIM * n + RIM] for f in flat]
+            before = None
+            for k in range(LAYERS):
+                wk = float(w[k])
+                strain = c0 + (c1 * wk + c2 * (wk * wk))
+                if k < LAYERS - 1:
+                    strain = strain + c3 * float((w[k + 1] - w[k]) ** 2)
+                twice = jnp.exp2(jnp.log(strain) * THIRD)
+                q_ref[k, at] = twice
+                r_ref[k, at] = dr + twice * (n0 + n1 * wk)
+                if k > 0:
+                    g_ref[k - 1, at] = 0.5 * (before + twice)
+                before = twice
+
+    def step(d, e, t, g, q, r):
+        d = e + (g if d is None else g * d)
+        return d, q * d + g * e, r * d + g * t
+
+    def from_surface(at):
+        d, e, t = None, q_ref[LAYERS - 1, at], r_ref[LAYERS - 1, at]
+        for k in range(LAYERS - 1):
+            j = LAYERS - 2 - k
+            d, e, t = step(d, e, t, g_ref[j, at], q_ref[j, at], r_ref[j, at])
+            if k % RESCALE == RESCALE - 1 and k < LAYERS - 2:
+                shrink = 1.0 / d
+                d, e, t = None, e * shrink, t * shrink
+        return d, e, t
+
+    def from_base(at):
+        d, e, t, product = None, q_ref[0, at], r_ref[0, at], None
+        for k in range(LAYERS - 1):
+            g = g_ref[k, at]
+            product = g if product is None else product * g
+            d, e, t = step(d, e, t, g, q_ref[k + 1, at], r_ref[k + 1, at])
+            if k % RESCALE == RESCALE - 1 and k < LAYERS - 2:
+                shrink = 1.0 / d
+                d, e, t, product = None, e * shrink, t * shrink, product * shrink
+        shrink = 1.0 / e
+        return t * shrink, product * shrink
+
+    for n, c in enumerate(main_copies()):
+        c.wait_recv()
+    driving, rate, friction, melt, trans, leakage, overburden, scale, ice, grounded = [field_local(i) for i in range(10)]
+    friction = friction * grounded
+    scale = scale * grounded
+    speed, drop = first_velocity(driving, rate, friction, ice)
+    early_rows = slice(0, local - RIM)
+    late_rows = slice(local - RIM, local)
+    viscosity(
+        coefficients(
+            [between(f) for f in shifts(speed)], [between(f) for f in shifts(drop)],
+            between(drop), between(driving), between(rate),
+        ),
+        0,
+    )
+    early_down = from_surface(early_rows)
+    early_up = from_base(early_rows)
+    trans_eff, source = sheet(speed + drop * float(w[0]), trans, melt, friction)
+
+    for region in range(2):
+        for dx, condition in ((1, both(is_low, below)), (-1, both(is_high, above))):
+
+            @pl.when(condition)
+            def _(dx=dx, region=region):
+                for c in edge_copies(dx, region):
+                    c.wait_recv()
+
+    fills = (0.0, 1.0, 0.0, 0.0, 0.0, 1.0, 0.0, 0.0, 0.0, 0.0)
+    halo = [field_halo(i, fill) for i, fill in enumerate(fills)]
+    h_driving, h_rate, h_friction, h_melt, h_trans, h_leakage, h_overburden, h_scale, h_ice, h_grounded = halo
+    h_friction = h_friction * h_grounded
+    h_scale = h_scale * h_grounded
+    h_speed, h_drop = first_velocity(h_driving, h_rate, h_friction, h_ice)
+    h_trans_eff, h_source = sheet(h_speed + h_drop * float(w[0]), h_trans, h_melt, h_friction)
+    valid = join([jnp.broadcast_to(has_halo, (RIM, wide)), jnp.ones((local, wide), jnp.bool_)])
+    leakage = join([h_leakage, leakage])
+    pressure = water_solve(
+        join([h_overburden, overburden]), join([h_trans_eff, trans_eff]), leakage, join([h_source, source]), valid
+    )
+    scale = join([h_scale, scale])
+    friction = scale * pressure
+
+    def around(h, f):
+        return join([f[local - RIM :], h, f[:RIM]])
+
+    def pick(f):
+        return late_tile(f[RIM : 2 * RIM], f[2 * RIM :], f[:RIM])
+
+    viscosity(
+        coefficients(
+            [pick(f) for f in shifts(around(h_speed, speed))], [pick(f) for f in shifts(around(h_drop, drop))],
+            pick(around(h_drop, drop)), pick(around(h_driving, driving)), pick(around(h_rate, rate)),
+        ),
+        local - RIM,
+    )
+    late_down = from_surface(late_rows)
+    down_d, down_e, down_t = [join(p) for p in zip(early_down, late_down)]
+
+    def arrange(f):
+        return join([between(f[RIM:]), pick(join([f[late_end:], f[: 2 * RIM]]))])
+
+    def restore(f):
+        pieces = [f[RIM * k : RIM * k + RIM] for k in range(tiles)]
+        pieces = pieces[-1:] + pieces
+        return join([pieces[0]] + [jnp.where(upper_sub, q, p) for p, q in zip(pieces[:-1], pieces[1:])])
+
+    late_end = local
+    base = arrange(friction * (0.5 / join([h_rate, rate])))
+    ice = join([h_ice, ice])
+    basal = down_t / (down_e + base * down_d)
+    sliding = restore(basal) * ice
+    trans_eff, source = sheet(sliding, join([h_trans, trans]), join([h_melt, melt]), friction)
+    pressure = water_solve(pressure, trans_eff, leakage, source, valid)
+
+    def mine(f):
+        return jnp.where(is_low, f[RIM : RIM + half], f[2 * RIM : 2 * RIM + half])
+
+    block = mine(pressure)
+    send_p[0] = block[:, :lanes]
+    send_p[1] = block[:, lanes:]
+    place = pl.ds(pl.multiple_of(jnp.where(is_low, 0, half), RIM), half)
+    side = number(is_high)
+
+    def result_copy(src, plane, m, where, k, target):
+        return pltpu.make_async_remote_copy(
+            src_ref=src, dst_ref=out.at[0, plane, where], send_sem=out_send.at[m], recv_sem=out_recv.at[plane, k],
+            device_id=target, device_id_type=MESH,
+        )
+
+    def water_copies():
+        return [
+            result_copy(send_p.at[1], strip, 3, place, side, {"sec": sectors, "gy": partner}),
+            result_copy(send_p.at[0], strip, 4, place, side, {"sec": sectors}),
+        ]
+
+    def own_copies():
+        return [result_copy(send_p.at[1], 0, 0, place, side, {"gy": partner})]
+
+    def ice_copies():
+        return [result_copy(results.at[n], n, n, place, side, {"gy": partner}) for n in range(3)]
+
+    await_credit(sends_last, 2, 2)
+    start(sends_last, water_copies())
+    start(is_water, own_copies())
+
+    @pl.when(is_water)
+    def _():
+        out[0, 0, place] = block[:, :lanes]
+
+    late_up = from_base(late_rows)
+    top, reach = [join(p) for p in zip(early_up, late_up)]
+    surface = mine(restore(top - base * basal * reach) * ice)
+
+    @pl.when(is_ice)
+    def _():
+        for n, f in enumerate((surface, mine(sliding), mine(scale) * block)):
+            out[0, n, place] = f[:, :lanes]
+            results[n] = f[:, lanes:]
+        for c in ice_copies():
+            c.start()
+
+    for c in main_copies():
+        c.wait_send()
+    for dx, condition in ((-1, below), (1, above)):
+        wait_send(condition, edge_copies(dx, gy))
+    wait_send(sends_last, water_copies())
+    wait_send(is_water, own_copies())
+    wait_send(is_ice, ice_copies())
+
+    other = pl.ds(pl.multiple_of(jnp.where(is_low, half, 0), RIM), half)
+
+    def await_result(condition, plane, where, k):
+        @pl.when(condition)
+        def _():
+            result_copy(send_p.at[0], plane, 0, where, k, {"gy": partner}).wait_recv()
+
+    await_result(sec >= 0, 0, other, 1 - side)
+    for plane in range(1, 3):
+        await_result(is_ice, plane, other, 1 - side)
+        for k in range(2):
+            await_result(is_water, plane, pl.ds(half * k, half), k)
+
+
+def narrow_map(nx, *args):
+    sectors, rows, lanes = args[0].shape
+    half = rows // 2
+    local = half + RIM
+    f32 = jnp.float32
+    vmem = pltpu.VMEM
+    dma = pltpu.SemaphoreType.DMA
+    return pl.pallas_call(
+        functools.partial(narrow_kernel, sectors, nx),
+        out_shape=pltpu.VMEM((1, sectors, rows, lanes), f32),
+        in_specs=[pl.BlockSpec(memory_space=pltpu.HBM)] * len(args),
+        out_specs=pl.BlockSpec(memory_space=pltpu.VMEM),
+        scratch_shapes=[
+            vmem((8, rows, lanes), f32),
+            vmem((2, rows, lanes), jnp.int32),
+            vmem((8, local, lanes), f32),
+            vmem((2, local, lanes), jnp.int32),
+            vmem((2, 8, RIM, lanes), f32),
+            vmem((2, 2, RIM, lanes), jnp.int32),
+            vmem((LAYERS, local, 2 * lanes), f32),
+            vmem((LAYERS, local, 2 * lanes), f32),
+            vmem((LAYERS, local, 2 * lanes), f32),
+            vmem((2, half, lanes), f32),
+            vmem((3, half, lanes), f32),
+            dma((2,)),
+            dma((6,)),
+            dma((6,)),
+            pltpu.SemaphoreType.REGULAR((3,)),
+            dma((5,)),
+            dma((sectors, 2)),
+        ],
+        compiler_params=pltpu.CompilerParams(collective_id=0, has_side_effects=True),
+    )(*args)
+
+
 def solution(mesh):
     spec = P(None, "gx", "gy")
+    nx, ny = mesh.shape["gx"], mesh.shape["gy"]
+    on_device = functools.partial(narrow_map, nx) if ny == 2 else functools.partial(wide_map, nx, ny)
     return jax.shard_map(
-        functools.partial(on_device, mesh.shape["gx"], mesh.shape["gy"]),
+        on_device,
         mesh=mesh,
         in_specs=(spec,) * 10,
         out_specs=P("sec", None, "gx", "gy"),

time: 9.81 us -> 8.82 us (0.90)
  the two profiles are of different devices: /device:TPU:14 before, /device:TPU:7 now
where the time goes in v2:
time: 8.82 us; the launch traced here: 8.65 us
  Pallas kernels  8.01 us (91%)
  local copies, waits for them, and re-layouts  0.62 us (7%)
    pallas_call x1, Pallas kernels, narrow_map(): pl.pallas_call(functools.partial(narrow_kernel, sectors, nx), out_shape=p...  8.01 us
    unnamed x1, local copies, waits for them, and re-layouts  0.62 us

profile of v2, /device:TPU:7, one launch (start us, length us, event | category | flops | bytes accessed | tf_op | source)
XLA Modules:
  0.0 8.6 jit_solution(7025607042868056331)
XLA Ops:
  0.0 8.0 %shard_map.100 = f32[1,3,32,128]{3,2,1,0:T(8,128)S(1)} custom-call(f32[3,32,128]{2,1,0:T(8,128)} %refs_0_.1, f32[3,32,128]{2,1,0:T(8,128)} %refs_1_.1, f32[3,32,128]{2,1,0:T(8,128)} %refs_2_.1, s32[3,32,128]{2,1,0:T(8,128)} %refs_3_.1, s32[3,32,128]{2,1,0:T(8,128)} %refs_4_.1, f32[3,32,128]{2,1,0:T(8,128)} %refs_5_.1, f32[3,32,128]{2,1,0:T(8,128)} %refs_6_.1, ...), custom_call_target="tpu_custom_call" | custom-call | tf_op jit(solution)/shard_map/pallas_call | solution.py:787
  8.0 0.6 %copy.12 = f32[1,3,32,128]{3,2,1,0:T(8,128)} copy(f32[1,3,32,128]{3,2,1,0:T(8,128)S(1)} %shard_map.100) | data formatting | bytes 98304
